TPU v7x, 32 devices: a whole 2x2x4 slice. The times are simulated.
32 devices in a mesh: row: 8 (over z, x), col: 4 (over y, core).
Axes of the slice: x: 2, y: 2, z: 4, core: 2. Of those that a mesh axis runs over, the one named last changes fastest.
Arguments:
- alignment: bfloat16 [256, 192, 256], P('row', 'col'), may hold values from -8 to 8
- alignment_mask: int32 [256, 192], P('row', 'col'), may hold values from 0 to 1, as said below
- residue_mask: int32 [192], replicated, may hold values from 0 to 1, as said below
- pair_features: bfloat16 [192, 192, 128], P('row', 'col'), may hold values from -6 to 6
- outer_product_left: bfloat16 [256, 32], replicated, may hold values from -0.375 to 0.375
- outer_product_right: bfloat16 [256, 32], replicated, may hold values from -0.375 to 0.375
- outer_proj: bfloat16 [1024, 128], replicated, may hold values from -0.1875 to 0.1875
- triangle_proj: bfloat16 [128, 512], replicated, may hold values from -0.5 to 0.5
- triangle_gate: bfloat16 [128, 128], replicated, may hold values from -0.5 to 0.5
- triangle_out: bfloat16 [128, 128], replicated, may hold values from -0.5 to 0.5
- transition_in: bfloat16 [128, 512], replicated, may hold values from -0.5 to 0.5
- transition_out: bfloat16 [512, 128], replicated, may hold values from -0.25 to 0.25
Outputs:
- pair_out: bfloat16 [192, 192, 128], P('row', 'col')
Inputs may be any that keep to these rules, and one draw needn't show every extreme that they name: `residue_mask`: masked residues scattered anywhere; at least one residue is masked and at least one takes part. `alignment_mask`: 0 wherever residue_mask is 0.
All inputs are finite; a program needn't handle non-finite values.
Results may differ from a plain program's by a relative error of at most 0.014.
Values may be sent and summed in bfloat16 or wider, within the bound.
No kernel may reach another device: no remote copies, remote signals or barrier semaphores. Data moves between devices by JAX's collectives and lax.ppermute only.
A program may use at most 64 MiB of HBM per device.

v0:
```python
import jax
import jax.numpy as jnp
from jax import lax
from jax.sharding import PartitionSpec as P

epsilon = 1e-05


def normalize(values):
    mean_value = jnp.mean(values, axis=-1, keepdims=True)
    centered = values - mean_value
    variance = jnp.mean(centered * centered, axis=-1, keepdims=True)
    return centered * lax.rsqrt(variance + epsilon)


def shards(
    alignment,
    alignment_mask,
    residue_mask,
    pair_features,
    outer_product_left,
    outer_product_right,
    outer_proj,
    triangle_proj,
    triangle_gate,
    triangle_out,
    transition_in,
    transition_out,
):
    block_rows, block_cols, channels = pair_features.shape
    inner = triangle_out.shape[0]
    narrow = outer_product_left.shape[1]
    mask_float = alignment_mask.astype(jnp.float32)
    normed = normalize(alignment.astype(jnp.float32)).astype(jnp.bfloat16)
    left_side = (
        jnp.dot(normed, outer_product_left, preferred_element_type=jnp.float32)
        * mask_float[..., None]
    ).astype(jnp.bfloat16)
    right_side = (
        jnp.dot(normed, outer_product_right, preferred_element_type=jnp.float32)
        * mask_float[..., None]
    ).astype(jnp.bfloat16)
    mask_wire = alignment_mask.astype(jnp.bfloat16)
    right_all, right_mask = (
        lax.all_gather(right_side, "row", axis=0, tiled=True),
        lax.all_gather(mask_wire, "row", axis=0, tiled=True),
    )
    left_rows, left_row_mask = (
        lax.all_gather(left_side, "col", axis=1, tiled=True),
        lax.all_gather(mask_wire, "col", axis=1, tiled=True),
    )
    left_all, left_mask = (
        lax.all_to_all(left_rows, "row", split_axis=1, concat_axis=0, tiled=True),
        lax.all_to_all(left_row_mask, "row", split_axis=1, concat_axis=0, tiled=True),
    )
    sequences = left_all.shape[0]
    contract = (((0,), (0,)), ((), ()))
    outer = lax.dot_general(
        left_all.reshape(sequences, block_rows * narrow),
        right_all.reshape(sequences, block_cols * narrow),
        contract,
        preferred_element_type=jnp.float32,
    )
    outer = (
        outer.reshape(block_rows, narrow, block_cols, narrow)
        .transpose(0, 2, 1, 3)
        .astype(jnp.bfloat16)
    )
    outer = outer.reshape(block_rows, block_cols, narrow * narrow)
    projected = jnp.dot(outer, outer_proj, preferred_element_type=jnp.float32)
    counts = lax.dot_general(left_mask, right_mask, contract, preferred_element_type=jnp.float32)
    first = (
        pair_features.astype(jnp.float32) + projected / jnp.maximum(counts, 1.0)[..., None]
    ).astype(jnp.bfloat16)
    normed_pair = normalize(first.astype(jnp.float32)).astype(jnp.bfloat16)
    projections = jnp.dot(normed_pair, triangle_proj, preferred_element_type=jnp.float32)
    row_mask = lax.dynamic_slice_in_dim(
        residue_mask, lax.axis_index("row") * block_rows, block_rows
    ).astype(jnp.float32)
    col_mask = lax.dynamic_slice_in_dim(
        residue_mask, lax.axis_index("col") * block_cols, block_cols
    ).astype(jnp.float32)
    pair_mask = (row_mask[:, None] * col_mask[None, :])[..., None]
    left_tri = (
        jax.nn.sigmoid(projections[..., :inner]) * projections[..., inner : 2 * inner] * pair_mask
    ).astype(jnp.bfloat16)
    right_tri = (
        jax.nn.sigmoid(projections[..., 2 * inner : 3 * inner])
        * projections[..., 3 * inner :]
        * pair_mask
    ).astype(jnp.bfloat16)
    right_cols = lax.all_gather(right_tri, "row", axis=0, tiled=True)
    right_rows = lax.all_to_all(right_cols, "col", split_axis=0, concat_axis=1, tiled=True)
    summed = jnp.einsum(
        "ikc,jkc->ijc",
        lax.all_gather(left_tri, "col", axis=1, tiled=True),
        right_rows,
        preferred_element_type=jnp.float32,
    )
    normed_sum = normalize(summed).astype(jnp.bfloat16)
    update = jax.nn.sigmoid(
        jnp.dot(normed_pair, triangle_gate, preferred_element_type=jnp.float32)
    ) * jnp.dot(normed_sum, triangle_out, preferred_element_type=jnp.float32)
    second = (first.astype(jnp.float32) + update).astype(jnp.bfloat16)
    normed_second = normalize(second.astype(jnp.float32)).astype(jnp.bfloat16)
    hidden_units = jnp.maximum(
        jnp.dot(normed_second, transition_in, preferred_element_type=jnp.float32), 0.0
    ).astype(jnp.bfloat16)
    return (
        second.astype(jnp.float32)
        + jnp.dot(hidden_units, transition_out, preferred_element_type=jnp.float32)
    ).astype(jnp.bfloat16)


def solution(mesh):
    placed = (
        P("row", "col", None),
        P("row", "col"),
        P(),
        P("row", "col", None),
        P(),
        P(),
        P(),
        P(),
        P(),
        P(),
        P(),
        P(),
    )
    return jax.shard_map(
        shards, mesh=mesh, in_specs=placed, out_specs=P("row", "col", None), check_vma=False
    )
```

profile of v0, /device:TPU:0, one launch (start us, length us, event | category | flops | bytes accessed | tf_op | source)
XLA Modules:
  0.0 276.2 jit_solution(16021958013082864905)
XLA Ops:
  6.5 0.8 fusion.48
  7.4 6.2 %all-gather = bf16[4,48,32]{1,2,0:T(8,128)(2,1)S(1)} all-gather(bf16[1,48,32]{1,2,0:T(8,128)(2,1)S(1)} %bitcast.93), channel_id=1, replica_groups=mesh['row'=8,'col'=4] {'col'}, dimensions={0}, use_global_device_ids=true | all-gather | bytes 15360 | tf_op jit(solution)/shard_map/all_gather | solution.py:50
  13.8 0.7 reshape.110
  14.5 6.2 %all-to-all-start.1 = ((bf16[8,2,384]{2,1,0:T(2,128)(2,1)}), bf16[8,2,384]{2,1,0:T(2,128)(2,1)S(1)}, u32[]{:S(2)}, u32[]{:S(2)}) async-start(bf16[8,2,384]{2,1,0:T(2,128)(2,1)} %reshape.110), calls=%async_computation.1 | async-start | bytes 24576 | tf_op jit(solution)/shard_map/all_to_all | solution.py:54
  20.8 1.4 convert_reduce_fusion
  22.7 0.7 fusion.16
  24.1 13.4 %all_gather.18 = bf16[32,192,32]{2,0,1:T(8,128)(2,1)} all-gather(bf16[32,48,32]{2,0,1:T(8,128)(2,1)S(1)} %copy.51), channel_id=1, replica_groups=mesh['row'=8,'col'=4] {'col'}, dimensions={1}, use_global_device_ids=true | all-gather | bytes 491520 | tf_op jit(solution)/shard_map/all_gather | solution.py:49
  37.4 0.7 fusion.17
  38.1 45.3 %all_gather.19 = bf16[256,48,32]{1,2,0:T(8,128)(2,1)S(1)} all-gather(bf16[32,48,32]{1,2,0:T(8,128)(2,1)S(1)} %fusion.17), channel_id=1, replica_groups=mesh['row'=8,'col'=4] {'row'}, dimensions={0}, use_global_device_ids=true | all-gather | bytes 884736 | tf_op jit(solution)/shard_map/all_gather | solution.py:45
  83.6 3.8 %reshape.108 = bf16[8,2,12288]{2,1,0:T(2,128)(2,1)} reshape(bf16[192,32,32]{2,1,0:T(8,128)(2,1)} %bitcast.89) | data formatting | bytes 786432
  87.4 2.4 copy.56
  89.8 3.6 %all-to-all-start = ((bf16[8,2,12288]{2,1,0:T(2,128)(2,1)}), bf16[8,2,12288]{2,1,0:T(2,128)(2,1)S(1)}, u32[]{:S(2)}, u32[]{:S(2)}) async-start(bf16[8,2,12288]{2,1,0:T(2,128)(2,1)} %reshape.108), calls=%async_computation | async-start | bytes 786432 | tf_op jit(solution)/shard_map/all_to_all | solution.py:53
  93.4 35.2 %all_gather.21 = bf16[256,48]{1,0:T(8,128)(2,1)S(1)} all-gather(bf16[32,48]{1,0:T(8,128)(2,1)S(1)} %get-tuple-element.7), channel_id=1, replica_groups=mesh['row'=8,'col'=4] {'row'}, dimensions={0}, use_global_device_ids=true | all-gather | bytes 27648 | tf_op jit(solution)/shard_map/all_gather | solution.py:46
  129.0 0.8 reshape.109
  130.4 1.0 reshape.93
  131.6 3.7 %convert_bitcast_fusion = bf16[24,48,32,32]{1,2,3,0:T(8,128)(2,1)} fusion(bf16[24,32,256,1]{2,1,3,0:T(8,128)(2,1)S(1)} %bitcast.90, bf16[48,32,256]{2,0,1:T(8,128)(2,1)S(1)} %copy-done.4), kind=kOutput, calls=%fused_computation | convolution fusion | flops 605159424 | bytes 3538944 | tf_op jit(solution)/shard_map/dot_general | solution.py:58
  135.3 17.8 %copy.57 = bf16[24,48,32,32]{3,2,1,0:T(8,128)(2,1)} copy(bf16[24,48,32,32]{1,2,3,0:T(8,128)(2,1)} %convert_bitcast_fusion) | data formatting | bytes 4718592 | tf_op jit(solution)/shard_map/convert_element_type | solution.py:67
  153.1 12.7 %reshape.95 = bf16[24,48,1024]{2,1,0:T(8,128)(2,1)S(1)} reshape(bf16[24,48,32,32]{3,2,1,0:T(8,128)(2,1)} %copy.57) | data formatting | bytes 4718592 | tf_op jit(solution)/shard_map/reshape | solution.py:69
  165.9 1.8 fusion.49
  168.7 1.2 fusion.22
  170.0 0.7 all-gather.6.cloned.1.call-update
  170.7 48.0 %all-gather.4.cloned.1.call-done = bf16[192,48,128]{2,1,0:T(8,128)(2,1)} async-done(((bf16[24,48,128]{2,1,0:T(8,128)(2,1)}), bf16[192,48,128]{2,1,0:T(8,128)(2,1)}) %all-gather.4.cloned.1.call-update) | async-done | bytes 2359312 | tf_op jit(solution)/shard_map/all_gather | solution.py:92
  218.7 3.9 %all-to-all-start.2 = ((bf16[192,48,128]{2,1,0:T(8,128)(2,1)}), bf16[192,48,128]{2,1,0:T(8,128)(2,1)S(1)}, u32[]{:S(2)}, u32[]{:S(2)}) async-start(bf16[192,48,128]{2,1,0:T(8,128)(2,1)} %all-gather.4.cloned.1.call-done), calls=%async_computation.2 | async-start | bytes 4718592 | tf_op jit(solution)/shard_map/all_to_all | solution.py:93
  222.6 1.3 fusion.9
  223.9 18.8 %all-gather.6.cloned.1.call-done = bf16[24,192,128]{2,1,0:T(8,128)(2,1)} async-done(((bf16[24,48,128]{2,1,0:T(8,128)(2,1)}), bf16[24,192,128]{2,1,0:T(8,128)(2,1)}) %all-gather.6.cloned.1.call-update) | async-done | bytes 1179664 | tf_op jit(solution)/shard_map/all_gather | solution.py:96
  242.7 2.8 %copy.63 = bf16[24,192,128]{1,0,2:T(8,128)(2,1)} copy(bf16[24,192,128]{2,1,0:T(8,128)(2,1)} %all-gather.6.cloned.1.call-done) | data formatting | bytes 2359296 | tf_op jit(solution)/shard_map/all_gather | solution.py:96
  245.5 11.6 %all-to-all-done.2 = bf16[192,48,128]{2,1,0:T(8,128)(2,1)S(1)} async-done(((bf16[192,48,128]{2,1,0:T(8,128)(2,1)}), bf16[192,48,128]{2,1,0:T(8,128)(2,1)S(1)}, u32[]{:S(2)}, u32[]{:S(2)}) %all-to-all-start.2) | async-done | bytes 2359328 | tf_op jit(solution)/shard_map/all_to_all | solution.py:93
  257.1 2.1 copy.61
  259.2 3.8 %copy.62 = bf16[48,192,128]{1,0,2:T(8,128)(2,1)S(1)} copy(bf16[48,192,128]{2,1,0:T(8,128)(2,1)} %bitcast.86) | data formatting | bytes 4718592 | tf_op jit(solution)/shard_map/all_to_all | solution.py:93
  263.0 2.4 bitcast_reduce_fusion
  265.9 0.8 copy-done.2
  267.8 1.5 fusion.15
  (61 shorter events, 5.4 us)
Async XLA Ops:
  6.5 159.3 %copy-start = (bf16[1024,128]{1,0:T(8,128)(2,1)S(1)}, bf16[1024,128]{1,0:T(8,128)(2,1)}, u32[]{:S(2)}) copy-start(bf16[1024,128]{1,0:T(8,128)(2,1)} %param.18) | copy-start | bytes 786436
  6.5 15.7 %copy-start.3 = (bf16[32,48,256]{2,1,0:T(8,128)(2,1)S(1)}, bf16[32,48,256]{2,1,0:T(8,128)(2,1)}, u32[]{:S(2)}) copy-start(bf16[32,48,256]{2,1,0:T(8,128)(2,1)} %param.12) | copy-start | bytes 2359300
  6.5 16.2 %copy-start.11 = (bf16[256,32]{0,1:T(8,128)(2,1)S(1)}, bf16[256,32]{0,1:T(8,128)(2,1)}, u32[]{:S(2)}) copy-start(bf16[256,32]{0,1:T(8,128)(2,1)} %param.16) | copy-start | bytes 49156
  14.5 75.3 %all-to-all-start.1 = ((bf16[8,2,384]{2,1,0:T(2,128)(2,1)}), bf16[8,2,384]{2,1,0:T(2,128)(2,1)S(1)}, u32[]{:S(2)}, u32[]{:S(2)}) async-start(bf16[8,2,384]{2,1,0:T(2,128)(2,1)} %reshape.110), calls=%async_computation.1 | async-start | bytes 24576 | tf_op jit(solution)/shard_map/all_to_all | solution.py:54
  23.4 14.0 %copy-start.12 = (bf16[256,32]{0,1:T(8,128)(2,1)S(1)}, bf16[256,32]{0,1:T(8,128)(2,1)}, u32[]{:S(2)}) copy-start(bf16[256,32]{0,1:T(8,128)(2,1)} %param.17) | copy-start | bytes 49156
  38.1 45.4 %copy-start.13 = (s32[192]{0:T(256)S(1)}, s32[192]{0:T(256)}, u32[]{:S(2)}) copy-start(s32[192]{0:T(256)} %param.14) | copy-start | bytes 2308
  89.8 39.2 %all-to-all-start = ((bf16[8,2,12288]{2,1,0:T(2,128)(2,1)}), bf16[8,2,12288]{2,1,0:T(2,128)(2,1)S(1)}, u32[]{:S(2)}, u32[]{:S(2)}) async-start(bf16[8,2,12288]{2,1,0:T(2,128)(2,1)} %reshape.108), calls=%async_computation | async-start | bytes 786432 | tf_op jit(solution)/shard_map/all_to_all | solution.py:53
  93.4 125.3 %all-gather.4.cloned.1.call-start = ((), (), s32[]{:S(2)}) async-start(), calls=%async_computation.3 | async-start | bytes 2654208 | tf_op jit(solution)/shard_map/all_gather | solution.py:92
  130.4 1.2 copy-start.4
  165.9 2.3 copy-start.6
  167.7 54.8 %copy-start.1 = (f32[24,48,128]{2,1,0:T(8,128)}, f32[24,48,128]{2,1,0:T(8,128)S(1)}, u32[]{:S(2)}) copy-start(f32[24,48,128]{2,1,0:T(8,128)S(1)} %get-tuple-element.10) | copy-start | bytes 1769476
  169.9 72.8 %all-gather.6.cloned.1.call-start = ((), (), s32[]{:S(2)}) async-start(), calls=%async_computation.4 | async-start | bytes 1474560 | tf_op jit(solution)/shard_map/all_gather | solution.py:96
  170.7 51.9 %copy-start.10 = (bf16[128,128]{1,0:T(8,128)(2,1)S(1)}, bf16[128,128]{1,0:T(8,128)(2,1)}, u32[]{:S(2)}) copy-start(bf16[128,128]{1,0:T(8,128)(2,1)} %param.20) | copy-start | bytes 98308
  218.7 38.4 %all-to-all-start.2 = ((bf16[192,48,128]{2,1,0:T(8,128)(2,1)}), bf16[192,48,128]{2,1,0:T(8,128)(2,1)S(1)}, u32[]{:S(2)}, u32[]{:S(2)}) async-start(bf16[192,48,128]{2,1,0:T(8,128)(2,1)} %all-gather.4.cloned.1.call-done), calls=%async_computation.2 | async-start | bytes 4718592 | tf_op jit(solution)/shard_map/all_to_all | solution.py:93
  265.6 1.1 copy-start.2
  265.6 1.2 copy-start.5
  265.6 1.2 copy-start.7
  266.9 0.9 copy-start.8
  266.9 1.0 copy-start.9
Sparse Core Ops, SparseCore 0:
  170.0 48.6 all-gather.3
  220.2 22.3 all-gather.5
where the time goes:
time: 277 us; the launch traced here: 276 us
  blocking collectives  100 us (36%)
  waiting for transfers between devices  79.1 us (29%)
  local copies, waits for them, and re-layouts  50.8 us (18%)
  starting transfers between devices  13.7 us (5%)
  between operations  13.7 us (5%)
  matrix products  13.2 us (5%)
  other arithmetic  5.45 us (2%)
    all_gather x1, waiting for transfers between devices, shards(): right_cols = lax.all_gather(right_tri, 'row', axis=0, tiled=True)  48 us
    all_gather x1, blocking collectives, shards(): lax.all_gather(right_side, 'row', axis=0, tiled=True)  45.3 us
    all_gather x1, blocking collectives, shards(): lax.all_gather(mask_wire, 'row', axis=0, tiled=True)  35.2 us
    all_gather x1, waiting for transfers between devices, shards(): lax.all_gather(left_tri, 'col', axis=1, tiled=True)  18.8 us
    convert_element_type x1, local copies, waits for them, and re-layouts, shards(): outer = outer.reshape(block_rows, narrow, block_cols, narrow).transpose(0...  17.8 us
    all_gather x1, blocking collectives, shards(): lax.all_gather(left_side, 'col', axis=1, tiled=True)  13.4 us
    reshape x1, local copies, waits for them, and re-layouts, shards(): outer = outer.reshape(block_rows, block_cols, narrow * narrow)  12.7 us
    all_to_all x1, waiting for transfers between devices, shards(): lax.all_to_all(right_cols, 'col', split_axis=0, concat_axis=1, tiled=True)  11.6 us
  transfers between devices with their start and end apart: 5, of which 3 were waited for; matrix products, arithmetic and copies ran while one was open for 5% of the time, Pallas kernels for 0%

commit v1 on v0

--- a/solution.py
+++ b/solution.py
@@ -90,7 +90,10 @@
         * pair_mask
     ).astype(jnp.bfloat16)
     right_cols = lax.all_gather(right_tri, "row", axis=0, tiled=True)
-    right_rows = lax.all_to_all(right_cols, "col", split_axis=0, concat_axis=1, tiled=True)
+    size = lax.axis_size("col")
+    blocks = jnp.stack(jnp.split(right_cols, size, axis=0), axis=0)
+    blocks = lax.all_to_all(blocks, "col", split_axis=0, concat_axis=0)
+    right_rows = jnp.concatenate(blocks, axis=1)
     summed = jnp.einsum(
         "ikc,jkc->ijc",
         lax.all_gather(left_tri, "col", axis=1, tiled=True),

time: 277 us -> 281 us (1.014)
    all_gather x1, waiting for transfers between devices: 18.8 us -> 14.1 us  [shards(): lax.all_gather(left_tri, 'col', axis=1, tiled=True)]
    reshape x0 -> x1, local copies, waits for them, and re-layouts: none -> 3.78 us  [shards(): right_rows = jnp.concatenate(blocks, axis=1)]
    all_to_all x2 -> x1, local copies, waits for them, and re-layouts: 5.89 us -> 2.13 us  [shards(): blocks = lax.all_to_all(blocks, 'col', split_axis=0, concat_axis=0)]
    all_to_all x1, waiting for transfers between devices: 11.6 us -> 15.4 us  [shards(): blocks = lax.all_to_all(blocks, 'col', split_axis=0, concat_axis=0)]
  transfers between devices with their start and end apart: 5 -> 5, of which waited for: 3 -> 3; matrix products, arithmetic and copies ran while one was open for 5% -> 7% of each run, Pallas kernels for 0% -> 0%
where the time goes in v1:
time: 281 us; the launch traced here: 279 us
  blocking collectives  100 us (36%)
  waiting for transfers between devices  78.2 us (28%)
  local copies, waits for them, and re-layouts  52.8 us (19%)
  starting transfers between devices  13.9 us (5%)
  between operations  13.7 us (5%)
  matrix products  13.3 us (5%)
  other arithmetic  7.17 us (3%)
    all_gather x1, waiting for transfers between devices, shards(): right_cols = lax.all_gather(right_tri, 'row', axis=0, tiled=True)  48 us
    all_gather x1, blocking collectives, shards(): lax.all_gather(right_side, 'row', axis=0, tiled=True)  45.3 us
    all_gather x1, blocking collectives, shards(): lax.all_gather(mask_wire, 'row', axis=0, tiled=True)  35.2 us
    convert_element_type x1, local copies, waits for them, and re-layouts, shards(): outer = outer.reshape(block_rows, narrow, block_cols, narrow).transpose(0...  17.8 us
    all_to_all x1, waiting for transfers between devices, shards(): blocks = lax.all_to_all(blocks, 'col', split_axis=0, concat_axis=0)  15.4 us
    all_gather x1, waiting for transfers between devices, shards(): lax.all_gather(left_tri, 'col', axis=1, tiled=True)  14.1 us
    all_gather x1, blocking collectives, shards(): lax.all_gather(left_side, 'col', axis=1, tiled=True)  13.4 us
    reshape x1, local copies, waits for them, and re-layouts, shards(): outer = outer.reshape(block_rows, block_cols, narrow * narrow)  12.7 us
  transfers between devices with their start and end apart: 5, of which 3 were waited for; matrix products, arithmetic and copies ran while one was open for 7% of the time, Pallas kernels for 0%

profile of v1, /device:TPU:0, one launch (start us, length us, event | category | flops | bytes accessed | tf_op | source)
XLA Modules:
  0.0 279.2 jit_solution(5598558013396215464)
XLA Ops:
  6.5 0.8 fusion.48
  7.4 6.2 %all-gather = bf16[4,48,32]{1,2,0:T(8,128)(2,1)S(1)} all-gather(bf16[1,48,32]{1,2,0:T(8,128)(2,1)S(1)} %bitcast.99), channel_id=1, replica_groups=mesh['row'=8,'col'=4] {'col'}, dimensions={0}, use_global_device_ids=true | all-gather | bytes 15360 | tf_op jit(solution)/shard_map/all_gather | solution.py:50
  13.8 0.7 reshape.118
  14.5 6.2 %all-to-all-start.1 = ((bf16[8,2,384]{2,1,0:T(2,128)(2,1)}), bf16[8,2,384]{2,1,0:T(2,128)(2,1)S(1)}, u32[]{:S(2)}, u32[]{:S(2)}) async-start(bf16[8,2,384]{2,1,0:T(2,128)(2,1)} %reshape.118), calls=%async_computation.1 | async-start | bytes 24576 | tf_op jit(solution)/shard_map/all_to_all | solution.py:54
  20.8 1.4 convert_reduce_fusion
  24.1 13.4 %all_gather.18 = bf16[32,192,32]{2,0,1:T(8,128)(2,1)} all-gather(bf16[32,48,32]{2,0,1:T(8,128)(2,1)S(1)} %copy.50), channel_id=1, replica_groups=mesh['row'=8,'col'=4] {'col'}, dimensions={1}, use_global_device_ids=true | all-gather | bytes 491520 | tf_op jit(solution)/shard_map/all_gather | solution.py:49
  38.1 45.3 %all_gather.19 = bf16[256,48,32]{1,2,0:T(8,128)(2,1)S(1)} all-gather(bf16[32,48,32]{1,2,0:T(8,128)(2,1)S(1)} %fusion.17), channel_id=1, replica_groups=mesh['row'=8,'col'=4] {'row'}, dimensions={0}, use_global_device_ids=true | all-gather | bytes 884736 | tf_op jit(solution)/shard_map/all_gather | solution.py:45
  83.6 3.8 %reshape.116 = bf16[8,2,12288]{2,1,0:T(2,128)(2,1)} reshape(bf16[192,32,32]{2,1,0:T(8,128)(2,1)} %bitcast.95) | data formatting | bytes 786432
  87.4 2.4 copy.55
  89.8 3.6 %all-to-all-start = ((bf16[8,2,12288]{2,1,0:T(2,128)(2,1)}), bf16[8,2,12288]{2,1,0:T(2,128)(2,1)S(1)}, u32[]{:S(2)}, u32[]{:S(2)}) async-start(bf16[8,2,12288]{2,1,0:T(2,128)(2,1)} %reshape.116), calls=%async_computation | async-start | bytes 786432 | tf_op jit(solution)/shard_map/all_to_all | solution.py:53
  93.4 35.2 %all_gather.21 = bf16[256,48]{1,0:T(8,128)(2,1)S(1)} all-gather(bf16[32,48]{1,0:T(8,128)(2,1)S(1)} %get-tuple-element.11), channel_id=1, replica_groups=mesh['row'=8,'col'=4] {'row'}, dimensions={0}, use_global_device_ids=true | all-gather | bytes 27648 | tf_op jit(solution)/shard_map/all_gather | solution.py:46
  129.0 0.8 reshape.117
  130.4 1.0 reshape.99
  131.6 3.7 %convert_bitcast_fusion = bf16[24,48,32,32]{1,2,3,0:T(8,128)(2,1)} fusion(bf16[24,32,256,1]{2,1,3,0:T(8,128)(2,1)S(1)} %bitcast.96, bf16[48,32,256]{2,0,1:T(8,128)(2,1)S(1)} %copy-done.4), kind=kOutput, calls=%fused_computation | convolution fusion | flops 605159424 | bytes 3538944 | tf_op jit(solution)/shard_map/dot_general | solution.py:58
  135.3 17.8 %copy.56 = bf16[24,48,32,32]{3,2,1,0:T(8,128)(2,1)} copy(bf16[24,48,32,32]{1,2,3,0:T(8,128)(2,1)} %convert_bitcast_fusion) | data formatting | bytes 4718592 | tf_op jit(solution)/shard_map/convert_element_type | solution.py:67
  153.2 12.7 %reshape.101 = bf16[24,48,1024]{2,1,0:T(8,128)(2,1)S(1)} reshape(bf16[24,48,32,32]{3,2,1,0:T(8,128)(2,1)} %copy.56) | data formatting | bytes 4718592 | tf_op jit(solution)/shard_map/reshape | solution.py:69
  165.9 1.8 fusion.49
  168.7 1.2 fusion.22
  170.0 0.7 all-gather.6.cloned.1.call-update
  170.7 48.0 %all-gather.4.cloned.1.call-done = bf16[192,48,128]{2,1,0:T(8,128)(2,1)} async-done(((bf16[24,48,128]{2,1,0:T(8,128)(2,1)}), bf16[192,48,128]{2,1,0:T(8,128)(2,1)}) %all-gather.4.cloned.1.call-update) | async-done | bytes 2359312 | tf_op jit(solution)/shard_map/all_gather | solution.py:92
  218.7 2.0 slice_bitcast_fusion.3
  220.7 1.7 pad_maximum_fusion
  222.4 4.0 %all-to-all-start.2 = ((bf16[4,48,48,128]{3,2,1,0:T(8,128)(2,1)}), bf16[4,48,48,128]{3,2,1,0:T(8,128)(2,1)S(1)}, u32[]{:S(2)}, u32[]{:S(2)}) async-start(bf16[4,48,48,128]{3,2,1,0:T(8,128)(2,1)} %pad_maximum_fusion), calls=%async_computation.2 | async-start | bytes 4718592 | tf_op jit(solution)/shard_map/all_to_all | solution.py:95
  226.5 1.3 fusion.9
  227.8 14.1 %all-gather.6.cloned.1.call-done = bf16[24,192,128]{2,1,0:T(8,128)(2,1)} async-done(((bf16[24,48,128]{2,1,0:T(8,128)(2,1)}), bf16[24,192,128]{2,1,0:T(8,128)(2,1)}) %all-gather.6.cloned.1.call-update) | async-done | bytes 1179664 | tf_op jit(solution)/shard_map/all_gather | solution.py:99
  241.9 2.8 copy.62
  244.7 15.4 %all-to-all-done.2 = bf16[4,48,48,128]{3,2,1,0:T(8,128)(2,1)S(1)} async-done(((bf16[4,48,48,128]{3,2,1,0:T(8,128)(2,1)}), bf16[4,48,48,128]{3,2,1,0:T(8,128)(2,1)S(1)}, u32[]{:S(2)}, u32[]{:S(2)}) %all-to-all-start.2) | async-done | bytes 2359328 | tf_op jit(solution)/shard_map/all_to_all | solution.py:95
  260.1 2.1 copy.60
  262.2 3.8 %copy.61 = bf16[48,192,128]{1,0,2:T(8,128)(2,1)S(1)} copy(bf16[48,192,128]{2,1,0:T(8,128)(2,1)} %bitcast.92) | data formatting | bytes 4718592 | tf_op jit(solution)/shard_map/reshape | solution.py:96
  266.0 2.4 bitcast_reduce_fusion
  268.8 0.8 copy-done.2
  270.8 1.6 fusion.15
  (63 shorter events, 6.7 us)
Async XLA Ops:
  6.5 159.4 %copy-start = (bf16[1024,128]{1,0:T(8,128)(2,1)S(1)}, bf16[1024,128]{1,0:T(8,128)(2,1)}, u32[]{:S(2)}) copy-start(bf16[1024,128]{1,0:T(8,128)(2,1)} %param.18) | copy-start | bytes 786436
  6.5 15.7 %copy-start.3 = (bf16[32,48,256]{2,1,0:T(8,128)(2,1)S(1)}, bf16[32,48,256]{2,1,0:T(8,128)(2,1)}, u32[]{:S(2)}) copy-start(bf16[32,48,256]{2,1,0:T(8,128)(2,1)} %param.12) | copy-start | bytes 2359300
  6.5 16.2 %copy-start.11 = (bf16[256,32]{0,1:T(8,128)(2,1)S(1)}, bf16[256,32]{0,1:T(8,128)(2,1)}, u32[]{:S(2)}) copy-start(bf16[256,32]{0,1:T(8,128)(2,1)} %param.16) | copy-start | bytes 49156
  14.5 75.3 %all-to-all-start.1 = ((bf16[8,2,384]{2,1,0:T(2,128)(2,1)}), bf16[8,2,384]{2,1,0:T(2,128)(2,1)S(1)}, u32[]{:S(2)}, u32[]{:S(2)}) async-start(bf16[8,2,384]{2,1,0:T(2,128)(2,1)} %reshape.118), calls=%async_computation.1 | async-start | bytes 24576 | tf_op jit(solution)/shard_map/all_to_all | solution.py:54
  23.4 14.0 %copy-start.12 = (bf16[256,32]{0,1:T(8,128)(2,1)S(1)}, bf16[256,32]{0,1:T(8,128)(2,1)}, u32[]{:S(2)}) copy-start(bf16[256,32]{0,1:T(8,128)(2,1)} %param.17) | copy-start | bytes 49156
  38.1 45.4 %copy-start.13 = (s32[192]{0:T(256)S(1)}, s32[192]{0:T(256)}, u32[]{:S(2)}) copy-start(s32[192]{0:T(256)} %param.14) | copy-start | bytes 2308
  89.8 39.2 %all-to-all-start = ((bf16[8,2,12288]{2,1,0:T(2,128)(2,1)}), bf16[8,2,12288]{2,1,0:T(2,128)(2,1)S(1)}, u32[]{:S(2)}, u32[]{:S(2)}) async-start(bf16[8,2,12288]{2,1,0:T(2,128)(2,1)} %reshape.116), calls=%async_computation | async-start | bytes 786432 | tf_op jit(solution)/shard_map/all_to_all | solution.py:53
  93.4 125.3 %all-gather.4.cloned.1.call-start = ((), (), s32[]{:S(2)}) async-start(), calls=%async_computation.3 | async-start | bytes 2654208 | tf_op jit(solution)/shard_map/all_gather | solution.py:92
  130.4 1.2 copy-start.4
  165.9 2.3 copy-start.6
  167.8 58.7 %copy-start.1 = (f32[24,48,128]{2,1,0:T(8,128)}, f32[24,48,128]{2,1,0:T(8,128)S(1)}, u32[]{:S(2)}) copy-start(f32[24,48,128]{2,1,0:T(8,128)S(1)} %get-tuple-element.14) | copy-start | bytes 1769476
  169.9 72.0 %all-gather.6.cloned.1.call-start = ((), (), s32[]{:S(2)}) async-start(), calls=%async_computation.4 | async-start | bytes 1474560 | tf_op jit(solution)/shard_map/all_gather | solution.py:99
  222.4 4.0 %copy-start.10 = (bf16[128,128]{1,0:T(8,128)(2,1)S(1)}, bf16[128,128]{1,0:T(8,128)(2,1)}, u32[]{:S(2)}) copy-start(bf16[128,128]{1,0:T(8,128)(2,1)} %param.20) | copy-start | bytes 98308
  222.4 37.6 %all-to-all-start.2 = ((bf16[4,48,48,128]{3,2,1,0:T(8,128)(2,1)}), bf16[4,48,48,128]{3,2,1,0:T(8,128)(2,1)S(1)}, u32[]{:S(2)}, u32[]{:S(2)}) async-start(bf16[4,48,48,128]{3,2,1,0:T(8,128)(2,1)} %pad_maximum_fusion), calls=%async_computation.2 | async-start | bytes 4718592 | tf_op jit(solution)/shard_map/all_to_all | solution.py:95
  268.6 1.1 copy-start.2
  268.6 1.2 copy-start.5
  268.6 1.2 copy-start.7
  269.9 0.9 copy-start.8
  269.9 1.0 copy-start.9
Sparse Core Ops, SparseCore 0:
  170.1 48.6 all-gather.3
  220.3 21.6 all-gather.5
